TPU v7x, 256 devices: a whole 4x4x8 slice. The times are simulated.
256 devices in a mesh: dp: 64 (over y, z, core), tensor: 4 (over x).
Axes of the slice: x: 4, y: 4, z: 8, core: 2. Of those that a mesh axis runs over, the one named last changes fastest.
Arguments:
- activations: bfloat16 [32768, 8192], P('dp', 'tensor'), may hold values from -2000 to 2000
- norm_gain: float32 [8192], replicated, may hold values from 0.5 to 12
- w_query: bfloat16 [8192, 4096], P('dp', 'tensor'), may hold values from -0.0625 to 0.0625
- w_key: bfloat16 [8192, 512], P('dp', 'tensor'), may hold values from -0.0625 to 0.0625
- w_value: bfloat16 [8192, 512], P('dp', 'tensor'), may hold values from -0.0625 to 0.0625
- lengths: int32 [128], replicated, may hold values from 128 to 256
- languages: int32 [128], replicated, may hold values from 0 to 29
- lang_caps: int32 [30], replicated, may hold values from 128 to 256
- dest_shard: int32 [128], replicated, may hold values from 0 to 63, as said below
Outputs:
- attended: bfloat16 [32768, 4096], P('dp', 'tensor')
Inputs may be any that keep to these rules, and one draw needn't show every extreme that they name: `dest_shard`: every data shard receives exactly 2 documents.
All inputs are finite; a program needn't handle non-finite values.
Results may differ from a plain program's by a relative error of at most 0.007.
The roundings to bfloat16 on the way count: a program that leaves them out, or rounds other values in their place, can miss the bound.
Values may be sent and summed in bfloat16 or wider, within the bound.
A program may use at most 128 MiB of HBM per device.

v0:
```python
import math
import jax
import jax.numpy as jnp
from jax import lax
from jax.sharding import PartitionSpec as P

HEAD_WIDTH = 128
rope_base = 500000.0
norm_eps = 1e-05


def rotary_embedding(vectors, token_positions):
    half_width = vectors.shape[-1] // 2
    steps_range = jnp.arange(half_width, dtype=jnp.float32)
    frequency = jnp.exp(steps_range * (-2.0 * math.log(rope_base) / vectors.shape[-1]))
    angles = token_positions[..., None, None] * frequency
    cosine = jnp.cos(angles)
    sine_table = jnp.sin(angles)
    first_half = vectors[..., :half_width]
    second_half = vectors[..., half_width:]
    return jnp.concatenate(
        [
            first_half * cosine - second_half * sine_table,
            second_half * cosine + first_half * sine_table,
        ],
        axis=-1,
    )


def project(source_rows, norm_gain, w_query, w_key, w_value):
    gathered = lax.all_gather(source_rows, "tensor", axis=1, tiled=True)
    widened = gathered.astype(jnp.float32)
    row_scale = lax.rsqrt(jnp.mean(widened * widened, axis=1, keepdims=True) + norm_eps)
    normed = (widened * row_scale * norm_gain).astype(jnp.bfloat16)
    pieces = (
        lax.all_gather(w_query, "dp", axis=0, tiled=True),
        lax.all_gather(w_key, "dp", axis=0, tiled=True),
        lax.all_gather(w_value, "dp", axis=0, tiled=True),
    )
    return tuple(
        (
            jnp.dot(normed, weight_piece, preferred_element_type=jnp.float32)
            for weight_piece in pieces
        )
    )


def rotate_round(query_part, key_portion, value_portion, token_positions, head_dim):
    total_rows = query_part.shape[0]
    rotated_query = rotary_embedding(
        query_part.reshape(total_rows, -1, head_dim), token_positions
    ).reshape(total_rows, -1)
    rotated_key = rotary_embedding(
        key_portion.reshape(total_rows, -1, head_dim), token_positions
    ).reshape(total_rows, -1)
    return jnp.concatenate([rotated_query, rotated_key, value_portion], axis=1).astype(jnp.bfloat16)


def attend(packed, doc_lengths, query_width, key_width, head_dim, doc_max):
    total_rows = packed.shape[0]
    doc_total = total_rows // doc_max
    value_head_rows = key_width // head_dim
    heads_per_group = query_width // key_width
    queries = packed[:, :query_width].reshape(
        doc_total, doc_max, value_head_rows, heads_per_group, head_dim
    )
    key_rows = packed[:, query_width : query_width + key_width].reshape(
        doc_total, doc_max, value_head_rows, head_dim
    )
    value_rows = packed[:, query_width + key_width :].reshape(
        doc_total, doc_max, value_head_rows, head_dim
    )
    scores = jnp.einsum(
        "jqhgd,jkhd->jhgqk", queries, key_rows, preferred_element_type=jnp.float32
    ) / math.sqrt(head_dim)
    order_range = jnp.arange(doc_max)
    causal = order_range[:, None] >= order_range[None, :]
    scores = jnp.where(causal, scores, -jnp.inf)
    row_peak = jnp.max(scores, axis=-1, keepdims=True)
    exponent = jnp.exp(scores - row_peak)
    probability = (exponent / jnp.sum(exponent, axis=-1, keepdims=True)).astype(jnp.bfloat16)
    blended = jnp.einsum(
        "jhgqk,jkhd->jqhgd", probability, value_rows, preferred_element_type=jnp.float32
    )
    blended = blended.reshape(doc_total, doc_max, query_width)
    row_valid = order_range[None, :] < doc_lengths[:, None]
    result = jnp.where(row_valid[..., None], blended, 0.0)
    return result.reshape(total_rows, query_width).astype(jnp.bfloat16)


def local(
    activations, norm_gain, w_query, w_key, w_value, lengths, languages, lang_caps, dest_shard
):
    shard_count = lax.axis_size("dp")
    my_shard = lax.axis_index("dp")
    doc_count = lengths.shape[0]
    token_rows = activations.shape[0]
    rows_peer = token_rows // doc_count
    doc_max = rows_peer * shard_count
    docs_here = doc_count // shard_count
    head_dim = HEAD_WIDTH
    query_width = w_query.shape[1]
    key_width = w_key.shape[1]
    language_table = jnp.arange(lang_caps.shape[0])
    cap_of_doc = jnp.sum(
        jnp.where(languages[:, None] == language_table[None, :], lang_caps[None, :], 0), axis=1
    )
    capped = jnp.minimum(lengths, cap_of_doc)
    doc_order = jnp.arange(doc_count)
    same_dest = dest_shard[:, None] == dest_shard[None, :]
    doc_rank = jnp.sum(
        (same_dest & (doc_order[None, :] < doc_order[:, None])).astype(jnp.int32), axis=1
    )
    target_slot = dest_shard * docs_here + doc_rank
    holder = jnp.sum(
        jnp.where(doc_order[:, None] == target_slot[None, :], doc_order[None, :], 0), axis=1
    )
    mine = lax.dynamic_slice_in_dim(holder, my_shard * docs_here, docs_here)
    doc_lengths = jnp.take(capped, mine)
    holder_grid = jnp.transpose(holder.reshape(shard_count, docs_here))
    send_index = (
        holder_grid[:, None, :] * rows_peer + jnp.arange(rows_peer)[None, :, None]
    ).reshape(-1)
    outgoing = jnp.take(activations, send_index, axis=0).reshape(
        docs_here, rows_peer, shard_count, -1
    )
    arrived = lax.all_to_all(outgoing, "dp", split_axis=2, concat_axis=2, tiled=True)
    moved_rows = arrived.reshape(docs_here * doc_max, -1)
    query_part, key_portion, value_portion = project(moved_rows, norm_gain, w_query, w_key, w_value)
    token_positions = jnp.tile(jnp.arange(doc_max), docs_here).astype(jnp.float32)
    packed = rotate_round(query_part, key_portion, value_portion, token_positions, head_dim)
    return attend(packed, doc_lengths, query_width, key_width, head_dim, doc_max)


def solution(mesh):
    return jax.shard_map(
        local,
        mesh=mesh,
        in_specs=(
            P("dp", "tensor"),
            P(),
            P("dp", "tensor"),
            P("dp", "tensor"),
            P("dp", "tensor"),
            P(),
            P(),
            P(),
            P(),
        ),
        out_specs=P("dp", "tensor"),
        check_vma=False,
    )
```

profile of v0, /device:TPU:1, one launch (start us, length us, event | category | flops | bytes accessed | tf_op | source)
XLA Modules:
  0.0 453.7 jit_solution(18384676850716704676)
XLA Ops:
  6.5 1.0 convert_reduce_fusion
  7.5 0.7 multiply_add_fusion
  8.2 0.1 select_reduce_fusion
  8.3 0.1 mul.188
  8.7 0.1 copy.36
  8.8 3.3 gather_fusion.1
  12.2 3.8 copy_select_fusion
  16.0 64.1 %all_to_all.5 = bf16[2,4,64,2048]{3,1,0,2:T(4,128)(2,1)S(1)} all-to-all(bf16[2,4,64,2048]{3,1,0,2:T(4,128)(2,1)S(1)} %copy_select_fusion), channel_id=1, replica_groups=mesh['dp'=64,'tensor'=4] {'dp'}, dimensions={2} | all-to-all | bytes 4194304 | tf_op jit(solution)/shard_map/all_to_all | solution.py:127
  80.1 2.5 copy.38
  82.7 0.7 all-gather.9.cloned.1.call-update
  83.5 0.7 all-gather.7.cloned.1.call-update
  84.2 0.5 all-gather.11.cloned.1.call-update
  85.0 0.6 gather_fusion
  85.8 1.0 multiply_cosine_fusion
  86.8 77.9 %all-gather.5.cloned.1.call-done = bf16[512,8192]{1,0:T(8,128)(2,1)} async-done(((bf16[512,2048]{1,0:T(8,128)(2,1)}), bf16[512,8192]{1,0:T(8,128)(2,1)}) %all-gather.5.cloned.1.call-update) | async-done | bytes 8388624 | tf_op jit(solution)/shard_map/all_gather | solution.py:31
  164.7 5.1 %fusion = f32[512]{0:T(512)S(1)} fusion(bf16[512,8192]{1,0:T(8,128)(2,1)} %all-gather.5.cloned.1.call-done), kind=kLoop, calls=%fused_computation.4 | loop fusion | flops 12582400 | bytes 8390656 | tf_op jit(solution)/shard_map/reduce_sum | solution.py:33
  169.8 76.8 %all-gather.9.cloned.1.call-done = bf16[8192,128]{1,0:T(8,128)(2,1)} async-done(((bf16[128,128]{1,0:T(8,128)(2,1)}), bf16[8192,128]{1,0:T(8,128)(2,1)}) %all-gather.9.cloned.1.call-update) | async-done | bytes 2097168 | tf_op jit(solution)/shard_map/all_gather | solution.py:37
  246.6 6.5 %convolution_bitcast_fusion.1 = f32[512,1,128]{0,2,1:T(8,128)S(1)} fusion(bf16[8192,128]{1,0:T(8,128)(2,1)} %all-gather.9.cloned.1.call-done, bf16[512,8192]{1,0:T(8,128)(2,1)} %all-gather.5.cloned.1.call-done, f32[8192]{0:T(1024)S(1)} %copy-done.1, f32[512]{0:T(512)S(1)} %add_rsqrt_fusion), kind=kOutput, calls=%fused_computation.22 | convolution fusion | flops 1090519040 | bytes 10782720 | tf_op jit(solution)/shard_map/dot_general | solution.py:42
  253.1 0.6 fusion.19
  253.7 0.1 copy.49
  253.8 70.6 %all-gather.7.cloned.1.call-done = bf16[8192,128]{1,0:T(8,128)(2,1)} async-done(((bf16[128,128]{1,0:T(8,128)(2,1)}), bf16[8192,128]{1,0:T(8,128)(2,1)}) %all-gather.7.cloned.1.call-update) | async-done | bytes 2097168 | tf_op jit(solution)/shard_map/all_gather | solution.py:38
  324.4 6.4 %convolution_convert_fusion = bf16[512,128]{1,0:T(8,128)(2,1)S(1)} fusion(bf16[8192,128]{1,0:T(8,128)(2,1)} %all-gather.7.cloned.1.call-done, bf16[512,8192]{1,0:T(8,128)(2,1)} %all-gather.5.cloned.1.call-done, f32[8192]{0:T(1024)S(1)} %copy-done.1, f32[512]{0:T(512)S(1)} %add_rsqrt_fusion), kind=kOutput, calls=%fused_computation.23 | convolution fusion | flops 1090584576 | bytes 10651648 | tf_op jit(solution)/shard_map/dot_general | solution.py:42
  330.8 93.0 %all-gather.11.cloned.1.call-done = bf16[8192,1024]{1,0:T(8,128)(2,1)} async-done(((bf16[128,1024]{1,0:T(8,128)(2,1)}), bf16[8192,1024]{1,0:T(8,128)(2,1)}) %all-gather.11.cloned.1.call-update) | async-done | bytes 16777232 | tf_op jit(solution)/shard_map/all_gather | solution.py:36
  423.8 14.5 %convolution_bitcast_fusion = f32[64,8,8,128]{3,1,2,0:T(8,128)S(1)} fusion(bf16[8192,1024]{1,0:T(8,128)(2,1)} %all-gather.11.cloned.1.call-done, bf16[512,8192]{1,0:T(8,128)(2,1)} %all-gather.5.cloned.1.call-done, f32[8192]{0:T(1024)S(1)} %copy-done.1, f32[512]{0:T(512)S(1)} %add_rsqrt_fusion), kind=kOutput, calls=%fused_computation.21 | convolution fusion | flops 8606711808 | bytes 27297792 | tf_op jit(solution)/shard_map/dot_general | solution.py:42
  438.3 0.5 copy.51
  438.8 0.9 subtract_convert_fusion
  439.7 0.6 pad_maximum_fusion
  440.3 0.8 fusion.4
  441.0 0.9 fusion.3
  441.9 2.3 fusion.9
  444.2 1.7 copy.43
  445.9 1.2 fusion.5
  (35 shorter events, 0.8 us)
Async XLA Ops:
  6.5 2.3 copy-start
  6.5 158.2 %all-gather.5.cloned.1.call-start = ((), (), s32[]{:S(2)}) async-start(), calls=%async_computation.1 | async-start | bytes 10485760 | tf_op jit(solution)/shard_map/all_gather | solution.py:31
  80.1 4.6 %copy-start.2 = (s32[30]{0:T(128)S(1)}, s32[30]{0:T(128)}, u32[]{:S(2)}) copy-start(s32[30]{0:T(128)} %param.16) | copy-start | bytes 364
  80.1 4.6 %copy-start.3 = (s32[128]{0:T(128)S(1)}, s32[128]{0:T(128)}, u32[]{:S(2)}) copy-start(s32[128]{0:T(128)} %param.15) | copy-start | bytes 1540
  80.1 4.7 %copy-start.4 = (s32[128]{0:T(128)S(1)}, s32[128]{0:T(128)}, u32[]{:S(2)}) copy-start(s32[128]{0:T(128)} %param.14) | copy-start | bytes 1540
  82.7 164.0 %all-gather.9.cloned.1.call-start = ((), (), s32[]{:S(2)}) async-start(), calls=%async_computation.3 | async-start | bytes 2129920 | tf_op jit(solution)/shard_map/all_gather | solution.py:37
  83.4 241.0 %all-gather.7.cloned.1.call-start = ((), (), s32[]{:S(2)}) async-start(), calls=%async_computation.2 | async-start | bytes 2129920 | tf_op jit(solution)/shard_map/all_gather | solution.py:38
  84.2 339.6 %all-gather.11.cloned.1.call-start = ((), (), s32[]{:S(2)}) async-start(), calls=%async_computation.4 | async-start | bytes 17039360 | tf_op jit(solution)/shard_map/all_gather | solution.py:36
  86.8 159.8 %copy-start.1 = (f32[8192]{0:T(1024)S(1)}, f32[8192]{0:T(1024)}, u32[]{:S(2)}) copy-start(f32[8192]{0:T(1024)} %param.10) | copy-start | bytes 98308
Sparse Core Ops, SparseCore 0:
  82.8 81.8 all-gather.4
  167.5 79.0 all-gather.8
  249.4 74.9 all-gather.6
  327.1 96.6 all-gather.10
where the time goes:
time: 454 us
  waiting for transfers between devices  320 us (70%)
  blocking collectives  64.1 us (14%)
  matrix products  30.4 us (7%)
  other arithmetic  16.2 us (4%)
  between operations  13.3 us (3%)
  local copies, waits for them, and re-layouts  9.25 us (2%)
    all_gather x1, waiting for transfers between devices, project(): lax.all_gather(w_query, 'dp', axis=0, tiled=True)  93 us
    all_gather x1, waiting for transfers between devices, project(): gathered = lax.all_gather(source_rows, 'tensor', axis=1, tiled=True)  77.9 us
    all_gather x1, waiting for transfers between devices, project(): lax.all_gather(w_key, 'dp', axis=0, tiled=True)  76.8 us
    all_gather x1, waiting for transfers between devices, project(): lax.all_gather(w_value, 'dp', axis=0, tiled=True)  70.6 us
    all_to_all x1, blocking collectives, local(): lax.all_to_all(outgoing, 'dp', split_axis=2, concat_axis=2, tiled=True)  64.1 us
    dot_general x3, matrix products, project(): jnp.dot(normed, weight_piece, preferred_element_type=jnp.float32)  27.4 us
  transfers between devices with their start and end apart: 4, of which 4 were waited for; matrix products, arithmetic and copies ran while one was open for 5% of the time, Pallas kernels for 0%

commit v1 on v0

--- a/solution.py
+++ b/solution.py
@@ -7,6 +7,14 @@
 HEAD_WIDTH = 128
 rope_base = 500000.0
 norm_eps = 1e-05
+
+
+def tiled_gather(value, axis, dim):
+    devices = lax.axis_size(axis)
+    repeats = [devices if d == dim else 1 for d in range(value.ndim)]
+    return lax.all_to_all(
+        jnp.tile(value, repeats), axis, split_axis=dim, concat_axis=dim, tiled=True
+    )
 
 
 def rotary_embedding(vectors, token_positions):
@@ -34,7 +42,7 @@
     normed = (widened * row_scale * norm_gain).astype(jnp.bfloat16)
     pieces = (
         lax.all_gather(w_query, "dp", axis=0, tiled=True),
-        lax.all_gather(w_key, "dp", axis=0, tiled=True),
+        tiled_gather(w_key, "dp", 0),
         lax.all_gather(w_value, "dp", axis=0, tiled=True),
     )
     return tuple(

time: 454 us -> 376 us (0.83)
  waiting for transfers between devices: 320 us -> 235 us
  starting transfers between devices: 0.12 us -> 6.11 us
    all_gather x1 -> x0, waiting for transfers between devices: 76.8 us -> none  [project(): lax.all_gather(w_key, 'dp', axis=0, tiled=True)]
    all_gather x1, waiting for transfers between devices: 77.9 us -> 70.6 us  [project(): gathered = lax.all_gather(source_rows, 'tensor', axis=1, tiled=True)]
    all_to_all x0 -> x1, starting transfers between devices: none -> 6.03 us  [tiled_gather(): lax.all_to_all(jnp.tile(value, repeats), axis, split_axis=dim, concat_axi...]
  transfers between devices with their start and end apart: 4 -> 4, of which waited for: 4 -> 3; matrix products, arithmetic and copies ran while one was open for 5% -> 6% of each run, Pallas kernels for 0% -> 0%
where the time goes in v1:
time: 376 us
  waiting for transfers between devices  235 us (62%)
  blocking collectives  64.1 us (17%)
  matrix products  30.6 us (8%)
  other arithmetic  16.2 us (4%)
  between operations  13.3 us (4%)
  local copies, waits for them, and re-layouts  11 us (3%)
  starting transfers between devices  6.11 us (2%)
    all_gather x1, waiting for transfers between devices, project(): lax.all_gather(w_query, 'dp', axis=0, tiled=True)  93.1 us
    all_gather x1, waiting for transfers between devices, project(): gathered = lax.all_gather(source_rows, 'tensor', axis=1, tiled=True)  70.6 us
    all_gather x1, waiting for transfers between devices, project(): lax.all_gather(w_value, 'dp', axis=0, tiled=True)  69.6 us
    all_to_all x1, blocking collectives, local(): lax.all_to_all(outgoing, 'dp', split_axis=2, concat_axis=2, tiled=True)  64.1 us
    dot_general x3, matrix products, project(): jnp.dot(normed, weight_piece, preferred_element_type=jnp.float32)  27.6 us
  transfers between devices with their start and end apart: 4, of which 3 were waited for; matrix products, arithmetic and copies ran while one was open for 6% of the time, Pallas kernels for 0%

profile of v1, /device:TPU:1, one launch (start us, length us, event | category | flops | bytes accessed | tf_op | source)
XLA Modules:
  0.0 376.2 jit_solution(10887657832484510054)
XLA Ops:
  6.5 1.0 convert_reduce_fusion
  7.5 0.7 multiply_add_fusion
  8.2 0.1 select_reduce_fusion
  8.3 0.1 mul.188
  8.7 0.1 copy.36
  8.8 3.3 gather_fusion.1
  12.2 3.8 %copy_select_fusion = bf16[2,4,64,2048]{3,1,0,2:T(4,128)(2,1)S(1)} fusion(bf16[2,4,64,2048]{3,2,1,0:T(8,128)(2,1)} %bitcast.61, pred[2,4,64]{1,0,2:T(4,128)(4,1)S(1)} %copy.36), kind=kLoop, calls=%fused_computation.16 | loop fusion | flops 1048576 | bytes 4194816 | tf_op jit(solution)/shard_map/jit(_take)/select_n | solution.py:132
  16.0 64.1 %all_to_all.14 = bf16[2,4,64,2048]{3,1,0,2:T(4,128)(2,1)S(1)} all-to-all(bf16[2,4,64,2048]{3,1,0,2:T(4,128)(2,1)S(1)} %copy_select_fusion), channel_id=1, replica_groups=mesh['dp'=64,'tensor'=4] {'dp'}, dimensions={2} | all-to-all | bytes 4194304 | tf_op jit(solution)/shard_map/all_to_all | solution.py:135
  80.1 2.5 copy.38
  82.7 0.7 all-gather.6.cloned.1.call-update
  83.4 0.7 all-gather.8.cloned.1.call-update
  84.1 1.8 tile.2
  86.0 6.0 %all-to-all-start.1 = ((bf16[64,128,128]{2,1,0:T(8,128)(2,1)}), bf16[64,128,128]{2,1,0:T(8,128)(2,1)}, u32[]{:S(2)}, u32[]{:S(2)}) async-start(bf16[64,128,128]{2,1,0:T(8,128)(2,1)} %tile.2), calls=%async_computation.1 | async-start | bytes 4194304 | tf_op jit(solution)/shard_map/all_to_all | solution.py:15
  92.2 0.6 gather_fusion
  93.1 1.0 multiply_cosine_fusion
  94.1 70.6 %all-gather.4.cloned.1.call-done = bf16[512,8192]{1,0:T(8,128)(2,1)} async-done(((bf16[512,2048]{1,0:T(8,128)(2,1)}), bf16[512,8192]{1,0:T(8,128)(2,1)}) %all-gather.4.cloned.1.call-update) | async-done | bytes 8388624 | tf_op jit(solution)/shard_map/all_gather | solution.py:39
  164.7 5.1 %fusion = f32[512]{0:T(512)S(1)} fusion(bf16[512,8192]{1,0:T(8,128)(2,1)} %all-gather.4.cloned.1.call-done), kind=kLoop, calls=%fused_computation.4 | loop fusion | flops 12582400 | bytes 8390656 | tf_op jit(solution)/shard_map/reduce_sum | solution.py:41
  169.8 6.5 %convolution_bitcast_fusion.1 = f32[512,1,128]{0,2,1:T(8,128)S(1)} fusion(bf16[8192,128]{1,0:T(8,128)(2,1)} %bitcast.6, bf16[512,8192]{1,0:T(8,128)(2,1)} %all-gather.4.cloned.1.call-done, f32[8192]{0:T(1024)S(1)} %copy-done.2, f32[512]{0:T(512)S(1)} %add_rsqrt_fusion), kind=kOutput, calls=%fused_computation.22 | convolution fusion | flops 1090519040 | bytes 10782720 | tf_op jit(solution)/shard_map/dot_general | solution.py:50
  176.3 0.6 fusion.19
  176.9 0.1 copy.49
  177.0 69.6 %all-gather.6.cloned.1.call-done = bf16[8192,128]{1,0:T(8,128)(2,1)} async-done(((bf16[128,128]{1,0:T(8,128)(2,1)}), bf16[8192,128]{1,0:T(8,128)(2,1)}) %all-gather.6.cloned.1.call-update) | async-done | bytes 2097168 | tf_op jit(solution)/shard_map/all_gather | solution.py:46
  246.6 6.4 %convolution_convert_fusion = bf16[512,128]{1,0:T(8,128)(2,1)S(1)} fusion(bf16[8192,128]{1,0:T(8,128)(2,1)} %all-gather.6.cloned.1.call-done, bf16[512,8192]{1,0:T(8,128)(2,1)} %all-gather.4.cloned.1.call-done, f32[8192]{0:T(1024)S(1)} %copy-done.2, f32[512]{0:T(512)S(1)} %add_rsqrt_fusion), kind=kOutput, calls=%fused_computation.23 | convolution fusion | flops 1090584576 | bytes 10651648 | tf_op jit(solution)/shard_map/dot_general | solution.py:50
  253.0 93.1 %all-gather.8.cloned.1.call-done = bf16[8192,1024]{1,0:T(8,128)(2,1)} async-done(((bf16[128,1024]{1,0:T(8,128)(2,1)}), bf16[8192,1024]{1,0:T(8,128)(2,1)}) %all-gather.8.cloned.1.call-update) | async-done | bytes 16777232 | tf_op jit(solution)/shard_map/all_gather | solution.py:44
  346.1 14.7 %convolution_bitcast_fusion = f32[64,8,8,128]{3,1,2,0:T(8,128)S(1)} fusion(bf16[8192,1024]{1,0:T(8,128)(2,1)} %all-gather.8.cloned.1.call-done, bf16[512,8192]{1,0:T(8,128)(2,1)} %all-gather.4.cloned.1.call-done, f32[8192]{0:T(1024)S(1)} %copy-done.2, f32[512]{0:T(512)S(1)} %add_rsqrt_fusion), kind=kOutput, calls=%fused_computation.21 | convolution fusion | flops 8606711808 | bytes 27297792 | tf_op jit(solution)/shard_map/dot_general | solution.py:50
  360.9 0.5 copy.51
  361.3 0.9 subtract_convert_fusion
  362.2 0.6 pad_maximum_fusion
  362.8 0.8 fusion.4
  363.6 0.9 fusion.3
  364.4 2.3 fusion.9
  366.7 1.7 copy.43
  368.4 1.2 fusion.5
  (37 shorter events, 0.7 us)
Async XLA Ops:
  6.5 2.3 copy-start
  6.5 158.2 %all-gather.4.cloned.1.call-start = ((), (), s32[]{:S(2)}) async-start(), calls=%async_computation.2 | async-start | bytes 10485760 | tf_op jit(solution)/shard_map/all_gather | solution.py:39
  80.1 4.0 %copy-start.1 = (bf16[128,128]{1,0:T(8,128)(2,1)S(1)}, bf16[128,128]{1,0:T(8,128)(2,1)}, u32[]{:S(2)}) copy-start(bf16[128,128]{1,0:T(8,128)(2,1)} %param.12) | copy-start | bytes 98308
  82.6 9.4 %copy-start.3 = (s32[30]{0:T(128)S(1)}, s32[30]{0:T(128)}, u32[]{:S(2)}) copy-start(s32[30]{0:T(128)} %param.16) | copy-start | bytes 364
  82.6 9.4 %copy-start.4 = (s32[128]{0:T(128)S(1)}, s32[128]{0:T(128)}, u32[]{:S(2)}) copy-start(s32[128]{0:T(128)} %param.15) | copy-start | bytes 1540
  82.6 9.5 %copy-start.5 = (s32[128]{0:T(128)S(1)}, s32[128]{0:T(128)}, u32[]{:S(2)}) copy-start(s32[128]{0:T(128)} %param.14) | copy-start | bytes 1540
  82.6 164.0 %all-gather.6.cloned.1.call-start = ((), (), s32[]{:S(2)}) async-start(), calls=%async_computation.3 | async-start | bytes 2129920 | tf_op jit(solution)/shard_map/all_gather | solution.py:46
  83.4 262.7 %all-gather.8.cloned.1.call-start = ((), (), s32[]{:S(2)}) async-start(), calls=%async_computation.4 | async-start | bytes 17039360 | tf_op jit(solution)/shard_map/all_gather | solution.py:44
  86.0 83.9 %all-to-all-start.1 = ((bf16[64,128,128]{2,1,0:T(8,128)(2,1)}), bf16[64,128,128]{2,1,0:T(8,128)(2,1)}, u32[]{:S(2)}, u32[]{:S(2)}) async-start(bf16[64,128,128]{2,1,0:T(8,128)(2,1)} %tile.2), calls=%async_computation.1 | async-start | bytes 4194304 | tf_op jit(solution)/shard_map/all_to_all | solution.py:15
  94.1 75.7 %copy-start.2 = (f32[8192]{0:T(1024)S(1)}, f32[8192]{0:T(1024)}, u32[]{:S(2)}) copy-start(f32[8192]{0:T(1024)} %param.10) | copy-start | bytes 98308
Sparse Core Ops, SparseCore 0:
  82.8 81.8 all-gather.3
  167.5 79.0 all-gather.5
  249.4 96.6 all-gather.7
